TPU v7x, 256 devices: a whole 4x4x8 slice. The times are simulated.
256 devices in a mesh: frame: 16 (over z, core), row: 16 (over x, y).
Axes of the slice: x: 4, y: 4, z: 8, core: 2. Of those that a mesh axis runs over, the one named last changes fastest.
Arguments:
- queries: bfloat16 [32, 64, 64, 2240], P('frame', 'row'), may hold values from -6 to 6
- keys: bfloat16 [32, 64, 64, 2240], P('frame', 'row'), may hold values from -12 to 12
- values: bfloat16 [32, 64, 64, 2240], P('frame', 'row'), may hold values from -12 to 12
- gate: bfloat16 [32, 64, 64, 2240], P('frame', 'row'), may hold values from -8 to 8
- conv_weight: float32 [3, 3, 2240], replicated, may hold values from -2 to 2
Outputs:
- mixed: bfloat16 [32, 64, 64, 2240], P('frame', 'row')
All inputs are finite; a program needn't handle non-finite values.
Results may differ from a plain program's by a relative error of at most 0.005.
Values may be sent and summed in bfloat16 or wider, within the bound.
A program may use at most 128 MiB of HBM per device.

v0:
```python
import jax
import jax.numpy as jnp
from jax import lax
from jax.sharding import Mesh
from jax.sharding import PartitionSpec as P

HEADS = 70
HEAD_DIM = 32
FRAME = ("frame_0", "frame_1")


def in_blocks(array, dim, devices):
    dims = array.shape
    blocks = array.reshape(*dims[:dim], devices, dims[dim] // devices, *dims[dim + 1 :])
    return jnp.moveaxis(blocks, dim, 0)


def sum_at_owner(array, axis, dim):
    devices = lax.axis_size(axis)
    blocks = lax.all_to_all(in_blocks(array, dim, devices), axis, 0, 0, tiled=True)
    return jnp.sum(blocks, axis=0)


def side_by_side(arrays, axis, dim, along):
    both = jnp.concatenate(arrays, axis=along)
    result, at, done = (sum_at_owner(both, axis, dim), 0, [])
    for a in arrays:
        done.append(lax.slice_in_dim(result, at, at + a.shape[along], axis=along))
        at += a.shape[along]
    return tuple(done)


def neutral_like(array, identity):
    return jax.tree.map(
        lambda a, e: jnp.broadcast_to(jnp.asarray(e, a.dtype), a.shape), array, identity
    )


def carried_in(array, axes, combine, identity):
    before = start = neutral_like(array, identity)
    subtotal = array
    for axis in reversed(axes):
        devices, position = (lax.axis_size(axis), lax.axis_index(axis))
        pieces = jax.tree.map(lambda part: lax.all_gather(part, axis), subtotal)
        inside, subtotal = (start, start)
        for k in range(devices):
            passed = k < position
            subtotal = combine(subtotal, jax.tree.map(lambda part: part[k], pieces))
            inside = jax.tree.map(lambda new, old: jnp.where(passed, new, old), subtotal, inside)
        before = combine(inside, before)
    return before


def gather_turned(arrays, axis, dims):
    turned = [jnp.moveaxis(a, dim, 0) for a, dim in zip(arrays, dims)]
    widths = [t[0].size for t in turned]
    both = jnp.concatenate([t.reshape(-1, w) for t, w in zip(turned, widths)], axis=1)
    result = lax.all_gather(both, axis, axis=0, tiled=True)
    blocks = jnp.split(result, [sum(widths[:k]) for k in range(1, len(widths))], axis=1)
    return tuple(
        (
            jnp.moveaxis(b.reshape(-1, *t.shape[1:]), 0, dim)
            for b, t, dim in zip(blocks, turned, dims)
        )
    )


def padded_2(array, sides, width):
    for axis, dim in sides:
        devices, length = (lax.axis_size(axis), array.shape[dim])
        up = [(i, (i + 1) % devices) for i in range(devices - 1)]
        down = [(j, i) for i, j in up]
        last = lax.slice_in_dim(array, length - width, length, axis=dim)
        leading = lax.slice_in_dim(array, 0, width, axis=dim)
        before = lax.ppermute(last, axis, up)
        after = lax.ppermute(leading, axis, down)
        array = jnp.concatenate([before, array, after], axis=dim)
    return array


def add_pair(earlier, later):
    return (earlier[0] + later[0], earlier[1] + later[1])


def per_device(queries, keys, values, gate, conv_weight):
    frames, rows, width, channels = queries.shape
    tokens = rows * width
    owner = jnp.arange(channels) // HEAD_DIM
    block = (owner[:, None] == owner[None, :]).astype(jnp.float32)
    head_sum = (owner[:, None] == jnp.arange(HEADS)[None, :]).astype(jnp.float32)
    kf = jax.nn.relu(keys).reshape(frames, tokens, channels)
    vf = values.reshape(frames, tokens, channels)

    def kv_state(pair):
        full = lax.dot_general(
            pair[0], pair[1], (((0,), (0,)), ((), ())), preferred_element_type=jnp.float32
        )
        return jnp.sum((full * block).reshape(HEADS, HEAD_DIM, channels), axis=0)

    partial_value = lax.map(kv_state, (kf, vf))
    norm_part = jnp.sum(kf, axis=1, dtype=jnp.float32)[:, None, :]
    partial_value, norm_part = side_by_side((partial_value, norm_part), "row", 2, 1)
    totals = (jnp.sum(partial_value, axis=0), jnp.sum(norm_part, axis=0))
    identity = (jnp.zeros_like(totals[0]), jnp.zeros_like(totals[1]))
    before = carried_in(totals, FRAME, add_pair, identity)
    states = before[0][None] + jnp.cumsum(partial_value, axis=0)
    zsum = before[1][None] + jnp.cumsum(norm_part, axis=0)
    states, zsum = gather_turned((states, zsum), "row", (2, 2))

    def read_frame(items):
        query, state, zrow = items
        qf = jax.nn.relu(query).astype(jnp.float32).reshape(tokens, channels)
        blocked = jnp.tile(state, (HEADS, 1)) * block
        numer = jnp.dot(qf, blocked, precision=lax.Precision.HIGHEST)
        per_head = jnp.dot(qf * zrow, head_sum, precision=lax.Precision.HIGHEST)
        denom = jnp.dot(per_head, head_sum.T, precision=lax.Precision.HIGHEST)
        return (numer / (denom + 1e-06)).reshape(rows, width, channels).astype(jnp.bfloat16)

    attended = lax.map(read_frame, (queries, states, zsum))
    padded = padded_2(attended, (("row", 1),), 1)
    mixes = []
    for b in range(3):
        total = jnp.zeros((frames, rows, width, channels), jnp.float32)
        for a in range(3):
            total = total + conv_weight[a, b] * padded[:, a : a + rows].astype(jnp.float32)
        mixes.append(total)
    column = jnp.zeros((frames, rows, 1, channels), jnp.float32)
    conv = mixes[1] + jnp.concatenate([column, mixes[0][:, :, :-1]], axis=2)
    conv = conv + jnp.concatenate([mixes[2][:, :, 1:], column], axis=2)
    return (conv * jax.nn.silu(gate.astype(jnp.float32))).astype(jnp.bfloat16)


def solution(mesh):
    split = Mesh(mesh.devices.reshape(8, 2, mesh.shape["row"]), ("frame_0", "frame_1", "row"))
    placed = (
        P(FRAME, "row", None, None),
        P(FRAME, "row", None, None),
        P(FRAME, "row", None, None),
        P(FRAME, "row", None, None),
        P(),
    )
    return jax.shard_map(
        per_device,
        mesh=split,
        in_specs=placed,
        out_specs=P(FRAME, "row", None, None),
        check_vma=False,
    )
```

profile of v0, /device:TPU:34, one launch (start us, length us, event | category | flops | bytes accessed | tf_op | source)
XLA Modules:
  0.0 275.1 jit_solution(16180616564460303154)
XLA Ops:
  0.0 2.0 broadcast_maximum_fusion
  2.0 0.4 copy-done.1
  2.4 0.5 convert_reduce_fusion
  2.9 35.6 %while.26 = (s32[]{:T(128)}, f32[2,32,2240]{2,1,0:T(8,128)S(1)}, bf16[2,256,2240]{2,1,0:T(8,128)(2,1)S(1)}, bf16[2,256,2240]{2,1,0:T(8,128)(2,1)}, s32[2240]{0:T(1024)S(1)}) while((s32[]{:T(128)}, f32[2,32,2240]{2,1,0:T(8,128)S(1)}, bf16[2,256,2240]{2,1,0:T(8,128)(2,1)S(1)}, bf16[2,256,2240]{2,1,0:T(8,128)(2,1)}, ...), condition=%wide.region_2.3_spmd.clone.clone, body=%wide.region_0.2_spmd.clone.sunk.clone | while | flops 2583992320 | bytes 43402308 | solution.py:100
  2.9 9.9 %convolution_select_fusion.3 = f32[2240,2240]{1,0:T(8,128)} fusion(s32[2240]{0:T(1024)S(1)} %get-tuple-element.328, bf16[2,256,2240]{2,1,0:T(8,128)(2,1)} %get-tuple-element.327, s32[]{:T(128)} %get-tuple-element.319, bf16[2,256,2240]{2,1,0:T(8,128)(2,1)S(1)} %get-tuple-element.326), kind=kOutput, calls=%fused_computation.3.clone.1.clone | convolution fusion | flops 2579046400 | bytes 22455296 | tf_op jit(solution)/shard_map/while/body/eval_jaxpr/dot_general | solution.py:95
  12.8 7.8 %reduce_sum.55 = f32[32,2240]{1,0:T(8,128)S(1)} reduce(f32[70,32,2240]{2,1,0:T(8,128)} %bitcast.123, f32[]{:T(128)} %constant.82.clone.1..sunk.1), dimensions={0}, to_apply=%region_1.1 | reduce | flops 4945920 | bytes 20357124 | tf_op jit(solution)/shard_map/while/body/eval_jaxpr/reduce_sum | solution.py:98
  20.7 9.9 %convolution_select_fusion.3 = f32[2240,2240]{1,0:T(8,128)} fusion(s32[2240]{0:T(1024)S(1)} %get-tuple-element.328, bf16[2,256,2240]{2,1,0:T(8,128)(2,1)} %get-tuple-element.327, s32[]{:T(128)} %get-tuple-element.319, bf16[2,256,2240]{2,1,0:T(8,128)(2,1)S(1)} %get-tuple-element.326), kind=kOutput, calls=%fused_computation.3.clone.1.clone | convolution fusion | flops 2579046400 | bytes 22455296 | tf_op jit(solution)/shard_map/while/body/eval_jaxpr/dot_general | solution.py:95
  30.7 7.8 %reduce_sum.55 = f32[32,2240]{1,0:T(8,128)S(1)} reduce(f32[70,32,2240]{2,1,0:T(8,128)} %bitcast.123, f32[]{:T(128)} %constant.82.clone.1..sunk.1), dimensions={0}, to_apply=%region_1.1 | reduce | flops 4945920 | bytes 20357124 | tf_op jit(solution)/shard_map/while/body/eval_jaxpr/reduce_sum | solution.py:98
  38.5 1.4 concatenate.24
  40.2 1.8 copy.33
  42.0 7.5 %all-to-all-start = ((f32[16,2,33,140]{3,1,2,0:T(2,128)}), f32[16,2,33,140]{3,1,2,0:T(2,128)S(1)}, u32[]{:S(2)}, u32[]{:S(2)}) async-start(f32[16,2,33,140]{3,1,2,0:T(2,128)} %copy.33), calls=%async_computation | async-start | bytes 2162688 | tf_op jit(solution)/shard_map/all_to_all | solution.py:20
  49.5 0.6 dynamic-slice
  50.1 0.7 dynamic-slice.1
  52.0 12.9 %all-to-all-done = f32[16,2,33,140]{3,1,2,0:T(2,128)S(1)} async-done(((f32[16,2,33,140]{3,1,2,0:T(2,128)}), f32[16,2,33,140]{3,1,2,0:T(2,128)S(1)}, u32[]{:S(2)}, u32[]{:S(2)}) %all-to-all-start) | async-done | bytes 591392 | tf_op jit(solution)/shard_map/all_to_all | solution.py:20
  64.9 0.5 reduce_sum.46
  65.8 2.4 all-reduce.2
  68.4 18.2 %all-reduce.3 = f32[1120]{0:T(1024)S(1)} all-reduce(f32[1120]{0:T(1024)S(1)} %get-tuple-element.217), channel_id=5, replica_groups=mesh['frame_0'=8,'frame_1'=2,'row'=16] {'frame_0'}, use_global_device_ids=true, to_apply=%add.3 | all-reduce | flops 1120 | bytes 8960
  86.7 1.9 all-gather
  88.6 23.7 %all-gather.2 = f32[256,140]{1,0:T(8,128)S(1)} all-gather(f32[32,140]{1,0:T(8,128)S(1)} %slice_add_fusion.5), channel_id=4, replica_groups=mesh['frame_0'=8,'frame_1'=2,'row'=16] {'frame_0'}, dimensions={0}, use_global_device_ids=true | all-gather | bytes 161280 | tf_op jit(solution)/shard_map/all_gather | solution.py:44
  112.6 24.8 %all-gather.4 = f32[16,140,66]{2,1,0:T(8,128)S(1)} all-gather(f32[1,140,66]{2,1,0:T(8,128)S(1)} %copy.35), channel_id=1, replica_groups=mesh['frame_0'=8,'frame_1'=2,'row'=16] {'row'}, dimensions={0}, use_global_device_ids=true | all-gather | bytes 628320 | tf_op jit(solution)/shard_map/all_gather | solution.py:58
  137.4 0.4 split.9
  137.8 0.4 copy.45
  138.2 0.4 copy.44
  138.5 106.1 %while.27 = (s32[]{:T(128)}, bf16[2,4,64,2240]{3,2,1,0:T(8,128)(2,1)}, bf16[2,4,64,2240]{3,2,1,0:T(8,128)(2,1)}, f32[2,32,2240]{2,1,0:T(8,128)S(1)}, f32[2,1,2240]{2,0,1:T(2,128)S(1)}, /*index=5*/s32[2240]{0:T(1024)S(1)}) while((s32[]{:T(128)}, bf16[2,4,64,2240]{3,2,1,0:T(8,128)(2,1)}, ...), condition=%wide.region_10.11_spmd.clone.clone.clone.clone, body=%wide.region_9.10_spmd.clone.clone.clone.sunk.clone | while | flops 16396566528 | bytes 96281672 | solution.py:119
  138.8 8.3 %compare_convert_fusion.3 = f32[2240,2240]{1,0:T(8,128)} fusion(s32[2240]{0:T(1024)S(1)} %get-tuple-element.346), kind=kLoop, calls=%fused_computation.10.clone.1.clone | loop fusion | flops 10035200 | bytes 20079360 | tf_op jit(solution)/shard_map/convert_element_type | solution.py:89
  147.1 15.7 %broadcast_multiply_fusion.3 = f32[70,32,2240]{2,1,0:T(8,128)} fusion(f32[70,32,2240]{2,1,0:T(8,128)} %bitcast.125, f32[32,2240]{1,0:T(8,128)S(1)} %dynamic-slice_bitcast_fusion.3), kind=kLoop, calls=%fused_computation.11.clone.1.clone | loop fusion | flops 5017600 | bytes 40427520 | tf_op jit(solution)/shard_map/while/body/eval_jaxpr/mul | solution.py:113
  162.7 1.3 dynamic-slice_maximum_fusion.3
  164.1 20.4 %fusion.84 = f32[256,2240]{0,1:T(8,128)S(1)} fusion(bf16[256,2240]{1,0:T(8,128)(2,1)S(1)} %bitcast.126, f32[2240,2240]{1,0:T(8,128)} %bitcast.124), kind=kOutput, calls=%fused_computation.109.clone.1.clone | convolution fusion | flops 15414067200 | bytes 23511040 | tf_op jit(solution)/shard_map/while/body/eval_jaxpr/dot_general | solution.py:114
  184.5 2.7 fusion.85
  187.2 2.6 fusion.86
  189.8 0.7 copy.56
  190.5 1.2 constant_dynamic-update-slice_fusion.3
  191.7 8.3 %compare_convert_fusion.3 = f32[2240,2240]{1,0:T(8,128)} fusion(s32[2240]{0:T(1024)S(1)} %get-tuple-element.346), kind=kLoop, calls=%fused_computation.10.clone.1.clone | loop fusion | flops 10035200 | bytes 20079360 | tf_op jit(solution)/shard_map/convert_element_type | solution.py:89
  200.0 15.7 %broadcast_multiply_fusion.3 = f32[70,32,2240]{2,1,0:T(8,128)} fusion(f32[70,32,2240]{2,1,0:T(8,128)} %bitcast.125, f32[32,2240]{1,0:T(8,128)S(1)} %dynamic-slice_bitcast_fusion.3), kind=kLoop, calls=%fused_computation.11.clone.1.clone | loop fusion | flops 5017600 | bytes 40427520 | tf_op jit(solution)/shard_map/while/body/eval_jaxpr/mul | solution.py:113
  215.7 1.3 dynamic-slice_maximum_fusion.3
  217.0 20.4 %fusion.84 = f32[256,2240]{0,1:T(8,128)S(1)} fusion(bf16[256,2240]{1,0:T(8,128)(2,1)S(1)} %bitcast.126, f32[2240,2240]{1,0:T(8,128)} %bitcast.124), kind=kOutput, calls=%fused_computation.109.clone.1.clone | convolution fusion | flops 15414067200 | bytes 23511040 | tf_op jit(solution)/shard_map/while/body/eval_jaxpr/dot_general | solution.py:114
  237.4 2.7 fusion.85
  240.2 2.6 fusion.86
  242.8 0.7 copy.56
  243.5 1.1 constant_dynamic-update-slice_fusion.3
  244.6 1.5 fusion.48
  246.1 2.5 collective-permute-start
  248.6 5.5 %collective-permute-start.1 = (bf16[2,1,64,2240]{3,2,1,0:T(8,128)(2,1)S(1)}, bf16[2,1,64,2240]{3,2,1,0:T(8,128)(2,1)S(1)}, u32[]{:S(2)}, u32[]{:S(2)}) collective-permute-start(bf16[2,1,64,2240]{3,2,1,0:T(8,128)(2,1)S(1)} %get-tuple-element.209), channel_id=1, source_target_pairs={{1,0},{2,1},{3,2},{4,3},{5,4},{6,5},{7,6},{8,7},{9,8},{10,9},{11,1... | collective-permute-start | bytes 1720328 | tf_op jit(solution)/shard_map/ppermute | solution.py:76
  254.3 5.7 %collective-permute-done = bf16[2,1,64,2240]{3,2,1,0:T(8,128)(2,1)S(1)} collective-permute-done((bf16[2,1,64,2240]{3,2,1,0:T(8,128)(2,1)S(1)}, bf16[2,1,64,2240]{3,2,1,0:T(8,128)(2,1)S(1)}, u32[]{:S(2)}, u32[]{:S(2)}) %collective-permute-start) | collective-permute-done | bytes 573472 | tf_op jit(solution)/shard_map/ppermute | solution.py:75
  260.0 1.5 collective-permute-done.1
  261.4 1.4 fusion.31
  262.9 3.9 %fusion.27 = (f32[2,4,63,2240]{3,2,1,0:T(8,128)S(1)}, f32[2,4,63,2240]{3,2,1,0:T(8,128)}) fusion(f32[2,4,64,2240]{3,2,1,0:T(8,128)S(1)} %get-tuple-element.206, f32[2,4,64,2240]{3,2,1,0:T(8,128)S(1)} %get-tuple-element.207, f32[2,4,64,2240]{3,2,1,0:T(8,128)S(1)} %get-tuple-element.205, f32[2240]{0:T(1024)S(1)} %get-tuple-element.172, ...), kind=kLoop, calls=%fused_computation.40 | loop fusion | flops 11289600 | bytes 36180480 | tf_op jit(solution)/shard_map/add | solution.py:125
  266.8 8.3 %fusion.29 = bf16[2,4,64,2240]{3,2,1,0:T(8,128)(2,1)} fusion(bf16[2,4,64,2240]{3,2,1,0:T(8,128)(2,1)} %param.12, f32[2,4,63,2240]{3,2,1,0:T(8,128)} %get-tuple-element.204, f32[2,4,63,2240]{3,2,1,0:T(8,128)S(1)} %get-tuple-element.203, f32[2240]{0:T(1024)S(1)} %get-tuple-element.175, f32[2240]{0:T(1024)S(1)} %get-tuple-element.176, ...), kind=kLoop, calls=%fused_computation.45 | loop fusion | flops 21790720 | bytes 17086720 | tf_op jit(solution)/shard_map/convert_element_type | solution.py:130
  (42 shorter events, 1.6 us)
Async XLA Ops:
  0.0 2.4 copy-start.1
  40.2 9.3 %copy-start.6 = (u32[256]{0:T(256)S(1)}, u32[256]{0:T(256)}, u32[]{:S(2)}) copy-start(u32[256]{0:T(256)} %constant.104) | copy-start | bytes 3076
  40.2 9.9 %copy-start.5 = (u32[256]{0:T(256)S(1)}, u32[256]{0:T(256)}, u32[]{:S(2)}) copy-start(u32[256]{0:T(256)} %constant.109) | copy-start | bytes 3076
  42.0 22.9 %all-to-all-start = ((f32[16,2,33,140]{3,1,2,0:T(2,128)}), f32[16,2,33,140]{3,1,2,0:T(2,128)S(1)}, u32[]{:S(2)}, u32[]{:S(2)}) async-start(f32[16,2,33,140]{3,1,2,0:T(2,128)} %copy.33), calls=%async_computation | async-start | bytes 2162688 | tf_op jit(solution)/shard_map/all_to_all | solution.py:20
  138.5 115.5 %copy-start.4 = (f32[3,3,2240]{2,1,0:T(4,128)S(1)}, f32[3,3,2240]{2,1,0:T(4,128)}, u32[]{:S(2)}) copy-start(f32[3,3,2240]{2,1,0:T(4,128)} %param.13) | copy-start | bytes 241924
  244.6 16.8 %copy-start = (bf16[2,4,64,2240]{3,2,1,0:T(8,128)(2,1)S(1)}, bf16[2,4,64,2240]{3,2,1,0:T(8,128)(2,1)}, u32[]{:S(2)}) copy-start(bf16[2,4,64,2240]{3,2,1,0:T(8,128)(2,1)} %get-tuple-element.73) | copy-start | bytes 6881284
  246.1 13.9 %collective-permute-start = (bf16[2,1,64,2240]{3,2,1,0:T(8,128)(2,1)S(1)}, bf16[2,1,64,2240]{3,2,1,0:T(8,128)(2,1)S(1)}, u32[]{:S(2)}, u32[]{:S(2)}) collective-permute-start(bf16[2,1,64,2240]{3,2,1,0:T(8,128)(2,1)S(1)} %get-tuple-element.208), channel_id=1, source_target_pairs={{0,1},{1,2},{2,3},{3,4},{4,5},{5,6},{6,7},{7,8},{8,9},{9,10},{10,1... | collective-permute-start | bytes 1720328 | tf_op jit(solution)/shard_map/ppermute | solution.py:75
  248.6 12.9 %collective-permute-start.1 = (bf16[2,1,64,2240]{3,2,1,0:T(8,128)(2,1)S(1)}, bf16[2,1,64,2240]{3,2,1,0:T(8,128)(2,1)S(1)}, u32[]{:S(2)}, u32[]{:S(2)}) collective-permute-start(bf16[2,1,64,2240]{3,2,1,0:T(8,128)(2,1)S(1)} %get-tuple-element.209), channel_id=1, source_target_pairs={{1,0},{2,1},{3,2},{4,3},{5,4},{6,5},{7,6},{8,7},{9,8},{10,9},{11,1... | collective-permute-start | bytes 1720328 | tf_op jit(solution)/shard_map/ppermute | solution.py:76
  260.0 2.9 %copy-start.2 = (bf16[2,1,64,2240]{3,2,1,0:T(8,128)(2,1)}, bf16[2,1,64,2240]{3,2,1,0:T(8,128)(2,1)S(1)}, u32[]{:S(2)}) copy-start(bf16[2,1,64,2240]{3,2,1,0:T(8,128)(2,1)S(1)} %collective-permute-done) | copy-start | bytes 1720324
  261.4 1.4 copy-start.3
where the time goes:
time: 280 us; the launch traced here: 275 us
  other arithmetic  83.5 us (30%)
  matrix products  71.2 us (25%)
  blocking collectives  71 us (25%)
  waiting for transfers between devices  20 us (7%)
  starting transfers between devices  15.4 us (6%)
  local copies, waits for them, and re-layouts  12.1 us (4%)
    dot_general x2, matrix products, read_frame(): numer = jnp.dot(qf, blocked, precision=lax.Precision.HIGHEST)  40.7 us
    mul x2, other arithmetic, read_frame(): blocked = jnp.tile(state, (HEADS, 1)) * block  31.3 us
    all_gather x2, blocking collectives, carried_in(): pieces = jax.tree.map(lambda part: lax.all_gather(part, axis), subtotal)  25.6 us
    all_gather x1, blocking collectives, gather_turned(): result = lax.all_gather(both, axis, axis=0, tiled=True)  24.8 us
    unnamed x2, blocking collectives  20.6 us
    dot_general x2, matrix products, kv_state(): lax.dot_general(pair[0], pair[1], (((0,), (0,)), ((), ())), preferred_ele...  19.9 us
    convert_element_type x2, other arithmetic, per_device(): block = (owner[:, None] == owner[None, :]).astype(jnp.float32)  16.6 us
    reduce_sum x2, other arithmetic, kv_state(): return jnp.sum((full * block).reshape(HEADS, HEAD_DIM, channels), axis=0)  15.7 us
  transfers between devices with their start and end apart: 3, of which 3 were waited for; matrix products, arithmetic and copies ran while one was open for 1% of the time, Pallas kernels for 0%

commit v1 on v0

v1 whole, which is shorter than its diff:
```python
import jax
import jax.numpy as jnp
from jax import lax
from jax.experimental import pallas as pl
from jax.experimental.pallas import tpu as pltpu
from jax.sharding import PartitionSpec as P

HEADS = 70
HEAD_DIM = 32
MESH = pl.DeviceIdType.MESH

GROUP = 256
PACKED = 2560
NORM_AT = 2304
CHUNK = 640
SIDE = 4


def sums_kernel(
    n_frame, n_row, q_ref, k_ref, v_ref, halo_ref, states_ref,
    k_buf, v_buf, part, rx, total, pair_rx, chip_total, chip_rx, before, mine,
    load_sem, halo_send, halo_recv, rs_send, rs_recv, pair_send, pair_recv,
    chip_send, chip_recv, ag_send, ag_recv, own_sem,
):
    frame = lax.axis_index("frame")
    row = lax.axis_index("row")
    core = lax.rem(frame, 2)
    chip = frame // 2
    n_chip = n_frame // 2
    partner = frame + 1 - 2 * core
    channels = k_buf.shape[-1]

    loads = []
    for f in range(2):
        loads.append(pltpu.make_async_copy(k_ref.at[f], k_buf.at[f], load_sem.at[0, f]))
        loads.append(pltpu.make_async_copy(v_ref.at[f], v_buf.at[f], load_sem.at[1, f]))
    for load in loads:
        load.start()

    barrier = pltpu.get_barrier_semaphore()

    @pl.loop(1, n_row)
    def _(i):
        pl.semaphore_signal(
            barrier, inc=1, device_id=(frame, lax.rem(row + i, n_row)), device_id_type=MESH
        )

    @pl.loop(1, n_chip)
    def _(i):
        pl.semaphore_signal(
            barrier, inc=1, device_id=(lax.rem(frame + 2 * i, n_frame), row), device_id_type=MESH
        )

    pl.semaphore_signal(barrier, inc=1, device_id=(partner, row), device_id_type=MESH)

    def halo(side, f):
        source, target = (3, row + 1) if side == 0 else (0, row - 1)
        return pltpu.make_async_remote_copy(
            src_ref=q_ref.at[f, source],
            dst_ref=halo_ref.at[side, f],
            send_sem=halo_send.at[side, f],
            recv_sem=halo_recv.at[side, f],
            device_id=(frame, target),
            device_id_type=MESH,
        )

    def halo_start(f):
        @pl.when(row < n_row - 1)
        def _():
            halo(0, f).start()

        @pl.when(row > 0)
        def _():
            halo(1, f).start()

    part[:, channels:] = jnp.zeros((64, PACKED - channels), part.dtype)

    def group(first, width, norms):
        ones = jnp.ones((k_buf.shape[1], 128), jnp.bfloat16)
        heads = width // HEAD_DIM
        lane = lax.broadcasted_iota(jnp.int32, (HEAD_DIM, width), 1) // HEAD_DIM
        slot = lax.broadcasted_iota(jnp.int32, (HEAD_DIM, 128), 1)
        first_head = first // HEAD_DIM
        compact = []
        new_norms = []
        for f in range(2):
            kf = jnp.maximum(k_buf[f, :, pl.ds(first, width)], 0)
            vf = jnp.concatenate([v_buf[f, :, pl.ds(first, width)], ones], axis=1)
            full = lax.dot_general(
                kf, vf, (((0,), (0,)), ((), ())), preferred_element_type=jnp.float32
            )
            state = jnp.zeros((HEAD_DIM, width), jnp.float32)
            norm = norms[f]
            for h in range(heads):
                rows = full[h * HEAD_DIM : (h + 1) * HEAD_DIM]
                state = jnp.where(lane == h, rows[:, :width], state)
                norm = jnp.where(slot == first_head + h, rows[:, width:], norm)
            compact.append(state)
            new_norms.append(norm)
        part[:, pl.ds(first, width)] = interleave(compact).astype(part.dtype)
        return tuple(new_norms)

    def interleave(pair):
        return jnp.concatenate(
            [pair[f][8 * q : 8 * q + 8] for q in range(SIDE) for f in range(2)], axis=0
        )

    for load in loads:
        load.wait()

    whole = channels // GROUP
    early = 3
    norms = tuple(jnp.zeros((HEAD_DIM, 128), jnp.float32) for _ in range(2))

    def step(g, norms):
        return group(pl.multiple_of(g * GROUP, GROUP), GROUP, norms)

    norms = lax.fori_loop(0, early, step, norms)
    pl.semaphore_wait(barrier, n_row - 1 + n_chip)
    halo_start(0)
    norms = lax.fori_loop(early, whole, step, norms)
    norms = group(whole * GROUP, channels - whole * GROUP, norms)
    part[:, NORM_AT : NORM_AT + 128] = interleave(norms).astype(part.dtype)

    def chunk(o):
        return (
            pl.ds(pl.multiple_of(16 * (o // SIDE), 16), 16),
            pl.ds(pl.multiple_of(CHUNK * lax.rem(o, SIDE), 128), CHUNK),
        )

    def scatter(i):
        peer = lax.rem(row + i, n_row)
        return pltpu.make_async_remote_copy(
            src_ref=part.at[chunk(peer)],
            dst_ref=rx.at[i],
            send_sem=rs_send.at[i],
            recv_sem=rs_recv.at[i],
            device_id=(frame, peer),
            device_id_type=MESH,
        )

    @pl.loop(1, n_row)
    def _(i):
        scatter(i).start()

    halo_start(1)

    sums = part[chunk(row)].astype(jnp.float32)

    def add(i, sums):
        scatter(i).wait_recv()
        return sums + rx[i].astype(jnp.float32)

    sums = lax.fori_loop(1, n_row, add, sums)
    even, odd = sums[:8], sums[8:]
    own_total = even + odd
    total[...] = own_total
    pair = pltpu.make_async_remote_copy(
        src_ref=total,
        dst_ref=pair_rx,
        send_sem=pair_send,
        recv_sem=pair_recv,
        device_id=(partner, row),
        device_id_type=MESH,
    )
    pair.start()
    pair.wait_recv()
    other = pair_rx[...]
    chip_total[...] = (own_total + other).astype(chip_total.dtype)

    def pass_on(i):
        return pltpu.make_async_remote_copy(
            src_ref=chip_total,
            dst_ref=chip_rx.at[i],
            send_sem=chip_send.at[i],
            recv_sem=chip_recv.at[i],
            device_id=(frame + 2 * i, row),
            device_id_type=MESH,
        )

    for i in range(1, n_chip):
        @pl.when(chip + i < n_chip)
        def _():
            pass_on(i).start()

    before[...] = jnp.where(core == 1, other, jnp.zeros_like(other))
    for i in range(1, n_chip):
        @pl.when(chip >= i)
        def _():
            pass_on(i).wait_recv()
            before[...] += chip_rx[i].astype(jnp.float32)

    first = before[...] + even
    mine[...] = jnp.concatenate([first, first + odd], axis=0).astype(mine.dtype)
    own = pltpu.make_async_copy(mine, states_ref.at[chunk(row)], own_sem)
    own.start()

    def gather(i):
        return pltpu.make_async_remote_copy(
            src_ref=mine,
            dst_ref=states_ref.at[chunk(row)],
            send_sem=ag_send.at[i],
            recv_sem=ag_recv.at[i],
            device_id=(frame, lax.rem(row + i, n_row)),
            device_id_type=MESH,
        )

    @pl.loop(1, n_row)
    def _(i):
        gather(i).start()

    @pl.loop(1, n_row)
    def _(i):
        gather(i).wait_recv()

    own.wait()

    @pl.when(row > 0)
    def _():
        for f in range(2):
            halo(0, f).wait_recv()
            halo(1, f).wait_send()

    @pl.when(row < n_row - 1)
    def _():
        for f in range(2):
            halo(1, f).wait_recv()
            halo(0, f).wait_send()

    pair.wait_send()
    for i in range(1, n_chip):
        @pl.when(chip + i < n_chip)
        def _():
            pass_on(i).wait_send()

    @pl.loop(1, n_row)
    def _(i):
        scatter(i).wait_send()
        gather(i).wait_send()


def mix_kernel(
    n_row, channels, q_ref, halo_ref, states_ref, norms_ref, gate_ref, weight_ref, out_ref, att
):
    row = lax.axis_index("row")
    g = pl.program_id(0)
    frames, rows, width, lanes = q_ref.shape
    inside = lax.broadcasted_iota(jnp.int32, (1, lanes), 1) < channels - g * lanes
    spread = (
        lax.broadcasted_iota(jnp.int32, (128, lanes), 0)
        == lax.broadcasted_iota(jnp.int32, (128, lanes), 1) // HEAD_DIM + g * (lanes // HEAD_DIM)
    ).astype(jnp.bfloat16)
    same = (
        lax.broadcasted_iota(jnp.int32, (lanes, lanes), 0) // HEAD_DIM
        == lax.broadcasted_iota(jnp.int32, (lanes, lanes), 1) // HEAD_DIM
    )
    states = states_ref[...].astype(jnp.float32)
    norms = jnp.dot(norms_ref[...], spread, preferred_element_type=jnp.float32)

    def blocks(packed, f):
        mine = jnp.concatenate(
            [packed[16 * q + 8 * f : 16 * q + 8 * f + 8] for q in range(SIDE)], axis=0
        )
        tiled = jnp.tile(mine, (lanes // HEAD_DIM, 1))
        return jnp.where(same, tiled, 0.0).astype(jnp.bfloat16)

    def attend(q, state, norm):
        qf = jnp.where(inside, jnp.maximum(q, 0), 0)
        numer = jnp.dot(qf, state, preferred_element_type=jnp.float32)
        denom = jnp.dot(qf, norm, preferred_element_type=jnp.float32)
        return (numer / (denom + 1e-6)).astype(jnp.bfloat16)

    column = lax.broadcasted_iota(jnp.int32, (width, lanes), 0)
    for f in range(frames):
        state, norm = blocks(states, f), blocks(norms, f)
        for r in range(rows):
            att[r + 1] = attend(q_ref[f, r], state, norm)
        top = attend(halo_ref[0, f], state, norm)
        att[0] = jnp.where(row > 0, top, jnp.zeros_like(top))
        bottom = attend(halo_ref[1, f], state, norm)
        att[rows + 1] = jnp.where(row < n_row - 1, bottom, jnp.zeros_like(bottom))
        for r in range(rows):
            three = [att[r + a].astype(jnp.float32) for a in range(3)]
            mixes = []
            for b in range(3):
                total = three[0] * weight_ref[0, b : b + 1]
                for a in range(1, 3):
                    total = total + three[a] * weight_ref[a, b : b + 1]
                mixes.append(total)
            left = jnp.where(column > 0, pltpu.roll(mixes[0], 1, 0), 0.0)
            right = jnp.where(column < width - 1, pltpu.roll(mixes[2], width - 1, 0), 0.0)
            conv = mixes[1] + left + right
            gate = gate_ref[f, r].astype(jnp.float32)
            out_ref[f, r] = (conv * (gate / (1.0 + jnp.exp(-gate)))).astype(out_ref.dtype)


def per_device(n_frame, n_row, queries, keys, values, gate, conv_weight):
    frames, rows, width, channels = queries.shape
    tokens = rows * width
    n_chip = n_frame // 2
    hbm = pl.BlockSpec(memory_space=pl.ANY)
    dma = pltpu.SemaphoreType.DMA
    halo, states = pl.pallas_call(
        lambda *refs: sums_kernel(n_frame, n_row, *refs),
        name="sums",
        out_shape=(
            jax.ShapeDtypeStruct((2, frames, width, channels), jnp.bfloat16),
            jax.ShapeDtypeStruct((64, PACKED), jnp.bfloat16),
        ),
        in_specs=[hbm] * 3,
        out_specs=(hbm, hbm),
        scratch_shapes=[
            pltpu.VMEM((frames, tokens, channels), jnp.bfloat16),
            pltpu.VMEM((frames, tokens, channels), jnp.bfloat16),
            pltpu.VMEM((64, PACKED), jnp.bfloat16),
            pltpu.VMEM((n_row, 16, CHUNK), jnp.bfloat16),
            pltpu.VMEM((8, CHUNK), jnp.float32),
            pltpu.VMEM((8, CHUNK), jnp.float32),
            pltpu.VMEM((8, CHUNK), jnp.bfloat16),
            pltpu.VMEM((n_chip, 8, CHUNK), jnp.bfloat16),
            pltpu.VMEM((8, CHUNK), jnp.float32),
            pltpu.VMEM((16, CHUNK), jnp.bfloat16),
            dma((2, 2)),
            dma((2, 2)),
            dma((2, 2)),
            dma((n_row,)),
            dma((n_row,)),
            dma,
            dma,
            dma((n_chip,)),
            dma((n_chip,)),
            dma((n_row,)),
            dma((n_row,)),
            dma,
        ],
        compiler_params=pltpu.CompilerParams(collective_id=0, has_side_effects=True),
    )(
        queries,
        keys.reshape(frames, tokens, channels),
        values.reshape(frames, tokens, channels),
    )
    lanes = GROUP
    return pl.pallas_call(
        lambda *refs: mix_kernel(n_row, channels, *refs),
        name="mix",
        grid=(pl.cdiv(channels, lanes),),
        out_shape=jax.ShapeDtypeStruct(queries.shape, jnp.bfloat16),
        in_specs=[
            pl.BlockSpec((frames, rows, width, lanes), lambda g: (0, 0, 0, g)),
            pl.BlockSpec((2, frames, width, lanes), lambda g: (0, 0, 0, g)),
            pl.BlockSpec((64, lanes), lambda g: (0, g)),
            pl.BlockSpec((64, 128), lambda g: (0, NORM_AT // 128)),
            pl.BlockSpec((frames, rows, width, lanes), lambda g: (0, 0, 0, g)),
            pl.BlockSpec((3, 3, lanes), lambda g: (0, 0, g)),
        ],
        out_specs=pl.BlockSpec((frames, rows, width, lanes), lambda g: (0, 0, 0, g)),
        scratch_shapes=[pltpu.VMEM((rows + 2, width, lanes), jnp.bfloat16)],
    )(queries, halo, states, states, gate, conv_weight)


def solution(mesh):
    split = P("frame", "row", None, None)
    sizes = (mesh.shape["frame"], mesh.shape["row"])
    return jax.shard_map(
        lambda *arrays: per_device(*sizes, *arrays),
        mesh=mesh,
        in_specs=(split, split, split, split, P()),
        out_specs=split,
        check_vma=False,
    )
```

time: 280 us -> 49.7 us (0.18)
  the two profiles are of different devices: /device:TPU:34 before, /device:TPU:8 now
where the time goes in v1:
time: 49.7 us; the launch traced here: 49.4 us
  Pallas kernels  49.4 us (99%)
    pallas_call x1, Pallas kernels, per_device(): pl.pallas_call(lambda *refs: sums_kernel(n_frame, n_row, *refs), name='su...  37 us
    pallas_call x1, Pallas kernels, per_device(): pl.pallas_call(lambda *refs: mix_kernel(n_row, channels, *refs), name='mi...  12.4 us

profile of v1, /device:TPU:8, one launch (start us, length us, event | category | flops | bytes accessed | tf_op | source)
XLA Modules:
  0.0 49.4 jit_solution(17481763627876675927)
XLA Ops:
  0.0 37.0 %sums.1 = (bf16[2,2,64,2240]{3,2,1,0:T(8,128)(2,1)}, bf16[64,2560]{1,0:T(8,128)(2,1)}) custom-call(bf16[2,4,64,2240]{3,2,1,0:T(8,128)(2,1)} %refs_0_.3, bf16[2,256,2240]{2,1,0:T(8,128)(2,1)} %bitcast.2, bf16[2,256,2240]{2,1,0:T(8,128)(2,1)} %bitcast.3), custom_call_target="tpu_custom_call" | custom-call | tf_op jit(solution)/shard_map/sums/pallas_call | solution.py:303
  37.0 12.4 %mix.1 = bf16[2,4,64,2240]{3,2,1,0:T(8,128)(2,1)} custom-call(bf16[2,4,64,2240]{3,2,1,0:T(8,128)(2,1)} %refs_0_.3, bf16[2,2,64,2240]{3,2,1,0:T(8,128)(2,1)} %get-tuple-element.7.refs_1_, bf16[64,2560]{1,0:T(8,128)(2,1)} %get-tuple-element.8.refs_2_.refs_3_, bf16[64,2560]{1,0:T(8,128)(2,1)} %get-tuple-element.8.refs_2_.refs_3_, ...), custom_call_target="tpu_custom_call" | custom-call | tf_op jit(solution)/shard_map/mix/pallas_call | solution.py:343

commit v2 on v1

v2 whole, which is shorter than its diff:
```python
import jax
import jax.numpy as jnp
from jax import lax
from jax.experimental import pallas as pl
from jax.experimental.pallas import tpu as pltpu
from jax.sharding import PartitionSpec as P

HEADS = 70
HEAD_DIM = 32
MESH = pl.DeviceIdType.MESH

GROUP = 256
PACKED = 2560
NORM_AT = 2304
CHUNK = 640
HALO_EARLY = 0
SIDE = 4


def mixer_kernel(
    n_frame, n_row, q_ref, k_ref, v_ref, gate_ref, weight_ref, out_ref,
    k_buf, v_buf, gate_buf, q_buf, silu_buf, weight_buf, halo_buf, att, states_buf, part, rx, total, pair_rx, chip_total, chip_rx, before, mine,
    load_sem, halo_send, halo_recv, rs_send, rs_recv, pair_send, pair_recv,
    chip_send, chip_recv, ag_send, ag_recv, own_sem, gate_sem, q_sem,
    weight_sem,
):
    frame = lax.axis_index("frame")
    row = lax.axis_index("row")
    core = lax.rem(frame, 2)
    chip = frame // 2
    n_chip = n_frame // 2
    partner = frame + 1 - 2 * core
    channels = k_buf.shape[-1]

    barrier = pltpu.get_barrier_semaphore()

    @pl.loop(1, n_row)
    def _(i):
        pl.semaphore_signal(
            barrier, inc=1, device_id=(frame, lax.rem(row + i, n_row)), device_id_type=MESH
        )

    @pl.loop(1, n_chip)
    def _(i):
        pl.semaphore_signal(
            barrier, inc=1, device_id=(lax.rem(frame + 2 * i, n_frame), row), device_id_type=MESH
        )

    pl.semaphore_signal(barrier, inc=1, device_id=(partner, row), device_id_type=MESH)

    stages = (0, 768, 1536, channels)
    loads = []
    for at, (low, high) in enumerate(zip(stages, stages[1:])):
        lanes = pl.ds(low, high - low)
        loads.append(
            [
                pltpu.make_async_copy(src.at[:, :, lanes], dst.at[:, :, lanes], load_sem.at[at, i])
                for i, (src, dst) in enumerate(((k_ref, k_buf), (v_ref, v_buf)))
            ]
        )
        for load in loads[-1]:
            load.start()
    gate_load = pltpu.make_async_copy(gate_ref, gate_buf, gate_sem)
    gate_load.start()
    q_load = pltpu.make_async_copy(q_ref, q_buf, q_sem)
    q_load.start()
    weight_load = pltpu.make_async_copy(weight_ref, weight_buf, weight_sem)
    weight_load.start()

    whole = channels // GROUP
    tail = channels - whole * GROUP

    def halo(side, g, lanes):
        source, target = (3, row + 1) if side == 0 else (0, row - 1)
        first = g * GROUP if lanes < GROUP else pl.multiple_of(g * GROUP, GROUP)
        cut = pl.ds(first, lanes)
        return pltpu.make_async_remote_copy(
            src_ref=q_buf.at[:, source, :, cut],
            dst_ref=halo_buf.at[side, :, :, cut],
            send_sem=halo_send.at[side, g],
            recv_sem=halo_recv.at[side, g],
            device_id=(frame, target),
            device_id_type=MESH,
        )

    def halo_start(low, high):
        def both(g, lanes):
            @pl.when(row < n_row - 1)
            def _():
                halo(0, g, lanes).start()

            @pl.when(row > 0)
            def _():
                halo(1, g, lanes).start()

        @pl.loop(low, min(high, whole))
        def _(g):
            both(g, GROUP)

        if high > whole:
            both(whole, tail)

    part[:, channels:] = jnp.zeros((64, PACKED - channels), part.dtype)

    def group(first, width, norms):
        ones = jnp.ones((k_buf.shape[1], 128), jnp.bfloat16)
        heads = width // HEAD_DIM
        lane = lax.broadcasted_iota(jnp.int32, (HEAD_DIM, width), 1) // HEAD_DIM
        slot = lax.broadcasted_iota(jnp.int32, (HEAD_DIM, 128), 1)
        first_head = first // HEAD_DIM
        compact = []
        new_norms = []
        for f in range(2):
            kf = jnp.maximum(k_buf[f, :, pl.ds(first, width)], 0)
            vf = jnp.concatenate([v_buf[f, :, pl.ds(first, width)], ones], axis=1)
            full = lax.dot_general(
                kf, vf, (((0,), (0,)), ((), ())), preferred_element_type=jnp.float32
            )
            state = jnp.zeros((HEAD_DIM, width), jnp.float32)
            norm = norms[f]
            for h in range(heads):
                rows = full[h * HEAD_DIM : (h + 1) * HEAD_DIM]
                state = jnp.where(lane == h, rows[:, :width], state)
                norm = jnp.where(slot == first_head + h, rows[:, width:], norm)
            compact.append(state)
            new_norms.append(norm)
        part[:, pl.ds(first, width)] = interleave(compact).astype(part.dtype)
        return tuple(new_norms)

    def interleave(pair):
        return jnp.concatenate(
            [pair[f][8 * q : 8 * q + 8] for q in range(SIDE) for f in range(2)], axis=0
        )

    def chunk(o):
        return (
            pl.ds(pl.multiple_of(16 * (o // SIDE), 16), 16),
            pl.ds(pl.multiple_of(CHUNK * lax.rem(o, SIDE), 128), CHUNK),
        )

    def scatter(peer):
        i = lax.rem(peer - row + n_row, n_row)
        return pltpu.make_async_remote_copy(
            src_ref=part.at[chunk(peer)],
            dst_ref=rx.at[i],
            send_sem=rs_send.at[i],
            recv_sem=rs_recv.at[i],
            device_id=(frame, peer),
            device_id_type=MESH,
        )

    def scatter_start(j):
        for i in range(SIDE):
            peer = lax.rem(row // SIDE + i + 1, SIDE) * SIDE + j
            if i < SIDE - 1:
                scatter(peer).start()
            else:
                @pl.when(peer != row)
                def _():
                    scatter(peer).start()

    norms = tuple(jnp.zeros((HEAD_DIM, 128), jnp.float32) for _ in range(2))

    def step(g, norms):
        return group(pl.multiple_of(g * GROUP, GROUP), GROUP, norms)

    for load in loads[0]:
        load.wait()
    norms = lax.fori_loop(0, 3, step, norms)
    for load in loads[1]:
        load.wait()
    norms = lax.fori_loop(3, 5, step, norms)
    pl.semaphore_wait(barrier, n_row - 1 + n_chip)
    scatter_start(0)
    scatter_start(1)
    for load in loads[2]:
        load.wait()
    norms = lax.fori_loop(5, 8, step, norms)
    scatter_start(2)
    norms = group(8 * GROUP, channels - 8 * GROUP, norms)
    part[:, NORM_AT : NORM_AT + 128] = interleave(norms).astype(part.dtype)
    scatter_start(3)

    @pl.when(row == 0)
    def _():
        halo_buf[0] = jnp.zeros_like(halo_buf[0])

    @pl.when(row == n_row - 1)
    def _():
        halo_buf[1] = jnp.zeros_like(halo_buf[1])

    gate_load.wait()
    frames, rows, width = q_buf.shape[:3]
    for f in range(frames):
        for r in range(rows):
            @pl.loop(0, width // 16)
            def _(i):
                cut = pl.ds(pl.multiple_of(16 * i, 16), 16)
                gate = gate_buf[f, r, cut].astype(jnp.float32)
                silu_buf[f, r, cut] = gate / (1.0 + jnp.exp(-gate))

    sums = part[chunk(row)].astype(jnp.float32)

    def add(i, sums):
        scatter(lax.rem(row + i, n_row)).wait_recv()
        return sums + rx[i].astype(jnp.float32)

    sums = lax.fori_loop(1, n_row, add, sums)
    q_load.wait()
    halo_start(0, HALO_EARLY)
    even, odd = sums[:8], sums[8:]
    own_total = even + odd
    total[...] = own_total
    pair = pltpu.make_async_remote_copy(
        src_ref=total,
        dst_ref=pair_rx,
        send_sem=pair_send,
        recv_sem=pair_recv,
        device_id=(partner, row),
        device_id_type=MESH,
    )
    pair.start()
    pair.wait_recv()
    other = pair_rx[...]
    chip_total[...] = (own_total + other).astype(chip_total.dtype)

    def pass_on(i):
        return pltpu.make_async_remote_copy(
            src_ref=chip_total,
            dst_ref=chip_rx.at[i],
            send_sem=chip_send.at[i],
            recv_sem=chip_recv.at[i],
            device_id=(frame + 2 * i, row),
            device_id_type=MESH,
        )

    for i in range(1, n_chip):
        @pl.when(chip + i < n_chip)
        def _():
            pass_on(i).start()

    before[...] = jnp.where(core == 1, other, jnp.zeros_like(other))
    for i in range(1, n_chip):
        @pl.when(chip >= i)
        def _():
            pass_on(i).wait_recv()
            before[...] += chip_rx[i].astype(jnp.float32)

    first = before[...] + even
    mine[...] = jnp.concatenate([first, first + odd], axis=0).astype(mine.dtype)
    own = pltpu.make_async_copy(mine, states_buf.at[chunk(row)], own_sem)
    own.start()

    def gather(i):
        return pltpu.make_async_remote_copy(
            src_ref=mine,
            dst_ref=states_buf.at[chunk(row)],
            send_sem=ag_send.at[i],
            recv_sem=ag_recv.at[i],
            device_id=(frame, lax.rem(row + i, n_row)),
            device_id_type=MESH,
        )

    @pl.loop(1, n_row)
    def _(i):
        gather(i).start()

    halo_start(HALO_EARLY, whole + 1)

    @pl.loop(1, n_row)
    def _(i):
        gather(i).wait_recv()

    own.wait()
    weight_load.wait()
    half = 128
    edge = lax.broadcasted_iota(jnp.int32, (8, half), 0)

    def attend(first, lanes, sources):
        heads = lanes // HEAD_DIM
        cut = pl.ds(first, lanes)
        spread = (
            lax.broadcasted_iota(jnp.int32, (128, lanes), 0)
            == lax.broadcasted_iota(jnp.int32, (128, lanes), 1) // HEAD_DIM + first // HEAD_DIM
        ).astype(jnp.bfloat16)
        same = (
            lax.broadcasted_iota(jnp.int32, (lanes, lanes), 0) // HEAD_DIM
            == lax.broadcasted_iota(jnp.int32, (lanes, lanes), 1) // HEAD_DIM
        )
        states = states_buf[:, cut].astype(jnp.float32)
        norms = jnp.dot(
            states_buf[:, NORM_AT : NORM_AT + 128], spread, preferred_element_type=jnp.float32
        )

        def blocks(packed, f):
            mine = jnp.concatenate(
                [packed[16 * q + 8 * f : 16 * q + 8 * f + 8] for q in range(SIDE)], axis=0
            )
            return jnp.where(same, jnp.tile(mine, (heads, 1)), 0.0).astype(jnp.bfloat16)

        for f in range(frames):
            state, norm = blocks(states, f), blocks(norms, f)
            for r, source in sources(f):
                qf = jnp.maximum(source[:, cut], 0)
                numer = jnp.dot(qf, state, preferred_element_type=jnp.float32)
                denom = jnp.dot(qf, norm, preferred_element_type=jnp.float32)
                att[f, r, :, cut] = numer / (denom + 1e-6)

    def mix(first, lanes, which):
        for low in range(0, lanes, half):
            wide = min(half, lanes - low)
            cut = pl.ds(first + low, wide)
            weights = [[weight_buf[a, b : b + 1, cut] for b in range(3)] for a in range(3)]
            for f in range(frames):
                for r in which:
                    three = [att[f, r + a, :, cut] for a in range(3)]
                    mixes = []
                    for b in range(3):
                        total = three[0] * weights[0][b]
                        for a in range(1, 3):
                            total = total + three[a] * weights[a][b]
                        mixes.append(total)
                    left = pltpu.roll(mixes[0], 1, 0)
                    first_rows = jnp.where(edge[:, :wide] > 0, left[:8], 0.0)
                    left = jnp.concatenate([first_rows, left[8:]], axis=0)
                    right = pltpu.roll(mixes[2], width - 1, 0)
                    last_rows = jnp.where(edge[:, :wide] < 7, right[-8:], 0.0)
                    right = jnp.concatenate([right[:-8], last_rows], axis=0)
                    conv = mixes[1] + left + right
                    out_ref[f, r, :, cut] = (conv * silu_buf[f, r, :, cut]).astype(out_ref.dtype)

    def inner(first, lanes):
        attend(first, lanes, lambda f: [(r + 1, q_buf.at[f, r]) for r in range(rows)])
        mix(first, lanes, range(1, rows - 1))

    def outer(g, first, lanes):
        @pl.when(row > 0)
        def _():
            halo(0, g, lanes).wait_recv()

        @pl.when(row < n_row - 1)
        def _():
            halo(1, g, lanes).wait_recv()

        attend(first, lanes, lambda f: [(0, halo_buf.at[0, f]), (rows + 1, halo_buf.at[1, f])])
        mix(first, lanes, (0, rows - 1))

    @pl.loop(0, whole)
    def _(g):
        inner(pl.multiple_of(g * GROUP, GROUP), GROUP)

    inner(whole * GROUP, tail)

    @pl.loop(0, whole)
    def _(g):
        outer(g, pl.multiple_of(g * GROUP, GROUP), GROUP)

    outer(whole, whole * GROUP, tail)

    @pl.loop(0, whole)
    def _(g):
        @pl.when(row < n_row - 1)
        def _():
            halo(0, g, GROUP).wait_send()

        @pl.when(row > 0)
        def _():
            halo(1, g, GROUP).wait_send()

    @pl.when(row < n_row - 1)
    def _():
        halo(0, whole, tail).wait_send()

    @pl.when(row > 0)
    def _():
        halo(1, whole, tail).wait_send()

    pair.wait_send()
    for i in range(1, n_chip):
        @pl.when(chip + i < n_chip)
        def _():
            pass_on(i).wait_send()

    @pl.loop(1, n_row)
    def _(i):
        scatter(lax.rem(row + i, n_row)).wait_send()
        gather(i).wait_send()


def per_device(n_frame, n_row, queries, keys, values, gate, conv_weight):
    frames, rows, width, channels = queries.shape
    tokens = rows * width
    n_chip = n_frame // 2
    groups = pl.cdiv(channels, GROUP)
    dma = pltpu.SemaphoreType.DMA
    flat = (frames, tokens, channels)
    arrays = (queries, keys.reshape(flat), values.reshape(flat), gate, conv_weight)
    return pl.pallas_call(
        lambda *refs: mixer_kernel(n_frame, n_row, *refs),
        name="mixer",
        out_shape=pltpu.VMEM(queries.shape, jnp.bfloat16),
        in_specs=[pl.BlockSpec(memory_space=pltpu.HBM)] * len(arrays),
        out_specs=pl.BlockSpec(memory_space=pltpu.VMEM),
        scratch_shapes=[
            pltpu.VMEM(flat, jnp.bfloat16),
            pltpu.VMEM(flat, jnp.bfloat16),
            pltpu.VMEM(gate.shape, jnp.bfloat16),
            pltpu.VMEM(queries.shape, jnp.bfloat16),
            pltpu.VMEM(queries.shape, jnp.float32),
            pltpu.VMEM(conv_weight.shape, jnp.float32),
            pltpu.VMEM((2, frames, width, channels), jnp.bfloat16),
            pltpu.VMEM((frames, rows + 2, width, channels), jnp.float32),
            pltpu.VMEM((64, PACKED), jnp.bfloat16),
            pltpu.VMEM((64, PACKED), jnp.bfloat16),
            pltpu.VMEM((n_row, 16, CHUNK), jnp.bfloat16),
            pltpu.VMEM((8, CHUNK), jnp.float32),
            pltpu.VMEM((8, CHUNK), jnp.float32),
            pltpu.VMEM((8, CHUNK), jnp.bfloat16),
            pltpu.VMEM((n_chip, 8, CHUNK), jnp.bfloat16),
            pltpu.VMEM((8, CHUNK), jnp.float32),
            pltpu.VMEM((16, CHUNK), jnp.bfloat16),
            dma((3, 2)),
            dma((2, groups)),
            dma((2, groups)),
            dma((n_row,)),
            dma((n_row,)),
            dma,
            dma,
            dma((n_chip,)),
            dma((n_chip,)),
            dma((n_row,)),
            dma((n_row,)),
            dma,
            dma,
            dma,
            dma,
        ],
        compiler_params=pltpu.CompilerParams(
            collective_id=0, has_side_effects=True, vmem_limit_bytes=40 << 20
        ),
    )(*(pltpu.with_memory_space_constraint(a, pltpu.HBM) for a in arrays))


def solution(mesh):
    split = P("frame", "row", None, None)
    sizes = (mesh.shape["frame"], mesh.shape["row"])
    return jax.shard_map(
        lambda *arrays: per_device(*sizes, *arrays),
        mesh=mesh,
        in_specs=(split, split, split, split, P()),
        out_specs=split,
        check_vma=False,
    )
```

time: 49.7 us -> 40.8 us (0.82)
  the two profiles are of different devices: /device:TPU:8 before, /device:TPU:34 now
where the time goes in v2:
time: 40.8 us; the launch traced here: 40.7 us
  Pallas kernels  39.3 us (96%)
  local copies, waits for them, and re-layouts  1.41 us (3%)
    pallas_call x1, Pallas kernels, per_device(): pl.pallas_call(lambda *refs: mixer_kernel(n_frame, n_row, *refs), name='m...  39.3 us
    unnamed x1, local copies, waits for them, and re-layouts  1.41 us

profile of v2, /device:TPU:34, one launch (start us, length us, event | category | flops | bytes accessed | tf_op | source)
XLA Modules:
  0.0 40.7 jit_solution(1875827315183312513)
XLA Ops:
  0.0 39.3 %mixer.1 = bf16[2,4,64,2240]{3,2,1,0:T(8,128)(2,1)S(1)} custom-call(bf16[2,4,64,2240]{3,2,1,0:T(8,128)(2,1)} %refs_0_.1, bf16[2,256,2240]{2,1,0:T(8,128)(2,1)} %bitcast.2, bf16[2,256,2240]{2,1,0:T(8,128)(2,1)} %bitcast.3, bf16[2,4,64,2240]{3,2,1,0:T(8,128)(2,1)} %refs_3_.1, f32[3,3,2240]{2,1,0:T(4,128)} %refs_4_.1), custom_call_target="tpu_custom_call" | custom-call | tf_op jit(solution)/shard_map/mixer/pallas_call | solution.py:398
  39.3 1.4 %copy.7 = bf16[2,4,64,2240]{3,2,1,0:T(8,128)(2,1)} copy(bf16[2,4,64,2240]{3,2,1,0:T(8,128)(2,1)S(1)} %mixer.1) | data formatting | bytes 4587520

commit v3 on v2

--- a/solution.py
+++ b/solution.py
@@ -13,13 +13,14 @@
 PACKED = 2560
 NORM_AT = 2304
 CHUNK = 640
-HALO_EARLY = 0
+HALO_EARLY = 1
+HALO_MORE = 2
 SIDE = 4
 
 
 def mixer_kernel(
     n_frame, n_row, q_ref, k_ref, v_ref, gate_ref, weight_ref, out_ref,
-    k_buf, v_buf, gate_buf, q_buf, silu_buf, weight_buf, halo_buf, att, states_buf, part, rx, total, pair_rx, chip_total, chip_rx, before, mine,
+    k_buf, v_buf, gate_buf, q_buf, silu_buf, weight_buf, halo_buf, att_00, att_01, att_10, att_11, states_buf, part, rx, total, pair_rx, chip_total, chip_rx, before, mine,
     load_sem, halo_send, halo_recv, rs_send, rs_recv, pair_send, pair_recv,
     chip_send, chip_recv, ag_send, ag_recv, own_sem, gate_sem, q_sem,
     weight_sem,
@@ -49,6 +50,7 @@
     pl.semaphore_signal(barrier, inc=1, device_id=(partner, row), device_id_type=MESH)
 
     stages = (0, 768, 1536, channels)
+    q_load = pltpu.make_async_copy(q_ref, q_buf, q_sem)
     loads = []
     for at, (low, high) in enumerate(zip(stages, stages[1:])):
         lanes = pl.ds(low, high - low)
@@ -60,10 +62,10 @@
         )
         for load in loads[-1]:
             load.start()
+        if at == 1:
+            q_load.start()
     gate_load = pltpu.make_async_copy(gate_ref, gate_buf, gate_sem)
     gate_load.start()
-    q_load = pltpu.make_async_copy(q_ref, q_buf, q_sem)
-    q_load.start()
     weight_load = pltpu.make_async_copy(weight_ref, weight_buf, weight_sem)
     weight_load.start()
 
@@ -171,6 +173,8 @@
         load.wait()
     norms = lax.fori_loop(3, 5, step, norms)
     pl.semaphore_wait(barrier, n_row - 1 + n_chip)
+    q_load.wait()
+    halo_start(0, HALO_EARLY)
     scatter_start(0)
     scatter_start(1)
     for load in loads[2]:
@@ -206,8 +210,6 @@
         return sums + rx[i].astype(jnp.float32)
 
     sums = lax.fori_loop(1, n_row, add, sums)
-    q_load.wait()
-    halo_start(0, HALO_EARLY)
     even, odd = sums[:8], sums[8:]
     own_total = even + odd
     total[...] = own_total
@@ -239,6 +241,7 @@
         def _():
             pass_on(i).start()
 
+    halo_start(HALO_EARLY, HALO_MORE)
     before[...] = jnp.where(core == 1, other, jnp.zeros_like(other))
     for i in range(1, n_chip):
         @pl.when(chip >= i)
@@ -265,7 +268,7 @@
     def _(i):
         gather(i).start()
 
-    halo_start(HALO_EARLY, whole + 1)
+    halo_start(HALO_MORE, whole + 1)
 
     @pl.loop(1, n_row)
     def _(i):
@@ -274,11 +277,24 @@
     own.wait()
     weight_load.wait()
     half = 128
+    att = ((att_00, att_01), (att_10, att_11))
     edge = lax.broadcasted_iota(jnp.int32, (8, half), 0)
 
-    def attend(first, lanes, sources):
+    def parity(g):
+        return g[1]
+
+    def start(g, lanes):
+        first = 2 * GROUP * g[0] + GROUP * g[1]
+        return first if lanes < GROUP else pl.multiple_of(first, GROUP)
+
+    def place(g, lanes):
+        return GROUP * g[0] if lanes < GROUP else pl.multiple_of(GROUP * g[0], GROUP)
+
+    def attend(g, lanes, sources):
         heads = lanes // HEAD_DIM
+        first = start(g, lanes)
         cut = pl.ds(first, lanes)
+        kept = pl.ds(place(g, lanes), lanes)
         spread = (
             lax.broadcasted_iota(jnp.int32, (128, lanes), 0)
             == lax.broadcasted_iota(jnp.int32, (128, lanes), 1) // HEAD_DIM + first // HEAD_DIM
@@ -298,22 +314,27 @@
             )
             return jnp.where(same, jnp.tile(mine, (heads, 1)), 0.0).astype(jnp.bfloat16)
 
-        for f in range(frames):
+        def frame_part(f):
             state, norm = blocks(states, f), blocks(norms, f)
             for r, source in sources(f):
                 qf = jnp.maximum(source[:, cut], 0)
                 numer = jnp.dot(qf, state, preferred_element_type=jnp.float32)
                 denom = jnp.dot(qf, norm, preferred_element_type=jnp.float32)
-                att[f, r, :, cut] = numer / (denom + 1e-6)
-
-    def mix(first, lanes, which):
-        for low in range(0, lanes, half):
-            wide = min(half, lanes - low)
-            cut = pl.ds(first + low, wide)
-            weights = [[weight_buf[a, b : b + 1, cut] for b in range(3)] for a in range(3)]
-            for f in range(frames):
+                att[parity(g)][f][r, :, kept] = numer / (denom + 1e-6)
+
+        return frame_part
+
+    def mix(g, lanes, which):
+        first, kept = start(g, lanes), place(g, lanes)
+
+        def frame_part(f):
+            for low in range(0, lanes, half):
+                wide = min(half, lanes - low)
+                cut = pl.ds(first + low, wide)
+                here = pl.ds(kept + low, wide)
+                weights = [[weight_buf[a, b : b + 1, cut] for b in range(3)] for a in range(3)]
                 for r in which:
-                    three = [att[f, r + a, :, cut] for a in range(3)]
+                    three = [att[parity(g)][f][r + a, :, here] for a in range(3)]
                     mixes = []
                     for b in range(3):
                         total = three[0] * weights[0][b]
@@ -329,11 +350,12 @@
                     conv = mixes[1] + left + right
                     out_ref[f, r, :, cut] = (conv * silu_buf[f, r, :, cut]).astype(out_ref.dtype)
 
-    def inner(first, lanes):
-        attend(first, lanes, lambda f: [(r + 1, q_buf.at[f, r]) for r in range(rows)])
-        mix(first, lanes, range(1, rows - 1))
-
-    def outer(g, first, lanes):
+        return frame_part
+
+    own_rows = lambda f: [(r + 1, q_buf.at[f, r]) for r in range(rows)]
+    halo_rows = lambda f: [(0, halo_buf.at[0, f]), (rows + 1, halo_buf.at[1, f])]
+
+    def arrived(g, lanes):
         @pl.when(row > 0)
         def _():
             halo(0, g, lanes).wait_recv()
@@ -342,20 +364,35 @@
         def _():
             halo(1, g, lanes).wait_recv()
 
-        attend(first, lanes, lambda f: [(0, halo_buf.at[0, f]), (rows + 1, halo_buf.at[1, f])])
-        mix(first, lanes, (0, rows - 1))
-
-    @pl.loop(0, whole)
-    def _(g):
-        inner(pl.multiple_of(g * GROUP, GROUP), GROUP)
-
-    inner(whole * GROUP, tail)
-
-    @pl.loop(0, whole)
-    def _(g):
-        outer(g, pl.multiple_of(g * GROUP, GROUP), GROUP)
-
-    outer(whole, whole * GROUP, tail)
+    def run(groups, sources, which):
+        attends = [attend(g, lanes, sources) for g, lanes in groups]
+        mixes = [mix(g, lanes, which) for g, lanes in groups]
+        steps = [(i, f) for i in range(len(groups)) for f in range(frames)]
+        for at, (i, f) in enumerate(steps):
+            attends[i](f)
+            if at > 0:
+                mixes[steps[at - 1][0]](steps[at - 1][1])
+        mixes[steps[-1][0]](steps[-1][1])
+
+    def pair_of(j):
+        return [((j, 0), GROUP), ((j, 1), GROUP)]
+
+    inner_rows, outer_rows = range(1, rows - 1), (0, rows - 1)
+
+    @pl.loop(0, whole // 2)
+    def _(j):
+        run(pair_of(j), own_rows, inner_rows)
+
+    run([((whole // 2, 0), tail)], own_rows, inner_rows)
+
+    @pl.loop(0, whole // 2)
+    def _(j):
+        arrived(2 * j, GROUP)
+        arrived(2 * j + 1, GROUP)
+        run(pair_of(j), halo_rows, outer_rows)
+
+    arrived(whole, tail)
+    run([((whole // 2, 0), tail)], halo_rows, outer_rows)
 
     @pl.loop(0, whole)
     def _(g):
@@ -409,7 +446,7 @@
             pltpu.VMEM(queries.shape, jnp.float32),
             pltpu.VMEM(conv_weight.shape, jnp.float32),
             pltpu.VMEM((2, frames, width, channels), jnp.bfloat16),
-            pltpu.VMEM((frames, rows + 2, width, channels), jnp.float32),
+            *(pltpu.VMEM((rows + 2, width, GROUP * 5), jnp.float32) for _ in range(4)),
             pltpu.VMEM((64, PACKED), jnp.bfloat16),
             pltpu.VMEM((64, PACKED), jnp.bfloat16),
             pltpu.VMEM((n_row, 16, CHUNK), jnp.bfloat16),

time: 40.8 us -> 39.6 us (0.971)
  the two profiles are of different devices: /device:TPU:34 before, /device:TPU:3 now
where the time goes in v3:
time: 39.6 us
  Pallas kernels  38.2 us (96%)
  local copies, waits for them, and re-layouts  1.41 us (4%)
    pallas_call x1, Pallas kernels, per_device(): pl.pallas_call(lambda *refs: mixer_kernel(n_frame, n_row, *refs), name='m...  38.2 us
    unnamed x1, local copies, waits for them, and re-layouts  1.41 us

profile of v3, /device:TPU:3, one launch (start us, length us, event | category | flops | bytes accessed | tf_op | source)
XLA Modules:
  0.0 39.6 jit_solution(17939867616456252513)
XLA Ops:
  0.0 38.2 %mixer.1 = bf16[2,4,64,2240]{3,2,1,0:T(8,128)(2,1)S(1)} custom-call(bf16[2,4,64,2240]{3,2,1,0:T(8,128)(2,1)} %refs_0_.1, bf16[2,256,2240]{2,1,0:T(8,128)(2,1)} %bitcast.2, bf16[2,256,2240]{2,1,0:T(8,128)(2,1)} %bitcast.3, bf16[2,4,64,2240]{3,2,1,0:T(8,128)(2,1)} %refs_3_.1, f32[3,3,2240]{2,1,0:T(4,128)} %refs_4_.1), custom_call_target="tpu_custom_call" | custom-call | tf_op jit(solution)/shard_map/mixer/pallas_call | solution.py:435
  38.2 1.4 %copy.7 = bf16[2,4,64,2240]{3,2,1,0:T(8,128)(2,1)} copy(bf16[2,4,64,2240]{3,2,1,0:T(8,128)(2,1)S(1)} %mixer.1) | data formatting | bytes 4587520

commit v4 on v3

--- a/solution.py
+++ b/solution.py
@@ -264,9 +264,10 @@
             device_id_type=MESH,
         )
 
-    @pl.loop(1, n_row)
-    def _(i):
-        gather(i).start()
+    steps = [(dx, dy) for dx in range(SIDE) for dy in range(SIDE) if dx or dy]
+    for dx, dy in sorted(steps, key=lambda d: ((0, 1, 3, 2)[d[0]], (0, 1, 3, 2)[d[1]])):
+        peer = lax.rem(row // SIDE + dx, SIDE) * SIDE + lax.rem(row + dy, SIDE)
+        gather(lax.rem(peer - row + n_row, n_row)).start()
 
     halo_start(HALO_MORE, whole + 1)
 

time: 39.6 us -> 39.1 us (0.987)
  the two profiles are of different devices: /device:TPU:3 before, /device:TPU:34 now
where the time goes in v4:
time: 39.1 us; the launch traced here: 38.8 us
  Pallas kernels  37.4 us (96%)
  local copies, waits for them, and re-layouts  1.41 us (4%)
    pallas_call x1, Pallas kernels, per_device(): pl.pallas_call(lambda *refs: mixer_kernel(n_frame, n_row, *refs), name='m...  37.4 us
    unnamed x1, local copies, waits for them, and re-layouts  1.41 us

profile of v4, /device:TPU:34, one launch (start us, length us, event | category | flops | bytes accessed | tf_op | source)
XLA Modules:
  0.0 38.8 jit_solution(10371677967552676347)
XLA Ops:
  0.0 37.4 %mixer.1 = bf16[2,4,64,2240]{3,2,1,0:T(8,128)(2,1)S(1)} custom-call(bf16[2,4,64,2240]{3,2,1,0:T(8,128)(2,1)} %refs_0_.1, bf16[2,256,2240]{2,1,0:T(8,128)(2,1)} %bitcast.2, bf16[2,256,2240]{2,1,0:T(8,128)(2,1)} %bitcast.3, bf16[2,4,64,2240]{3,2,1,0:T(8,128)(2,1)} %refs_3_.1, f32[3,3,2240]{2,1,0:T(4,128)} %refs_4_.1), custom_call_target="tpu_custom_call" | custom-call | tf_op jit(solution)/shard_map/mixer/pallas_call | solution.py:436
  37.4 1.4 %copy.7 = bf16[2,4,64,2240]{3,2,1,0:T(8,128)(2,1)} copy(bf16[2,4,64,2240]{3,2,1,0:T(8,128)(2,1)S(1)} %mixer.1) | data formatting | bytes 4587520
